TPU v7x, 512 devices: a whole 4x4x16 slice. The times are simulated.
512 devices in a mesh: row: 32 (over z, core), inner: 16 (over x, y).
Axes of the slice: x: 4, y: 4, z: 16, core: 2. Of those that a mesh axis runs over, the one named last changes fastest.
Arguments:
- a_left: bfloat16 [32, 64, 1024, 128], P('row', 'inner'), may hold values from -0.5 to 0.5
- a_right: bfloat16 [32, 64, 1024, 128], P('row', 'inner'), may hold values from -0.1875 to 0.1875
- a_rank: int32 [32, 64], P('row', 'inner'), may hold values from 16 to 128, as said below
- b_left: bfloat16 [64, 4, 1024, 128], P('inner', None, 'row'), may hold values from -6 to 6
- b_right: bfloat16 [64, 4, 1024, 128], P('inner', None, 'row'), may hold values from -0.0625 to 0.0625
- b_rank: int32 [64, 4], P('inner'), may hold values from 16 to 128, as said below
- c_rank: int32 [32, 4], P('row'), may hold values from 16 to 128, as said below
- probes: bfloat16 [1024, 128], replicated, may hold values from -6 to 6
Outputs:
- q_basis: bfloat16 [32, 1024, 512], P('row', 'inner')
- w_factor: bfloat16 [32, 1024, 512], P('row', 'inner')
Inputs may be any that keep to these rules, and one draw needn't show every extreme that they name: `a_rank`: A tile's factor columns at or beyond its rank are not used; some tile has rank 128 and some rank 128/8 in every draw. `b_rank`: likewise for the B tiles. `c_rank`: some C tile has target rank 128 and some 128/8 in every draw.
All inputs are finite; a program needn't handle non-finite values.
Results may differ from a plain program's by a relative error of at most 0.014.
Values may be sent and summed in bfloat16 or wider, within the bound.
A program may use at most 64 MiB of HBM per device.

v0:
```python
import jax
import jax.numpy as jnp
from jax import lax
from jax.sharding import PartitionSpec as P


def cholesky_inverse(gram_full):
    diag_mean = jnp.mean(jnp.diagonal(gram_full, axis1=1, axis2=2), axis=1)
    identity = jnp.eye(gram_full.shape[1], dtype=jnp.float32)
    gram_full = gram_full + 0.0001 * diag_mean[:, None, None] * identity[None]
    factor = jnp.linalg.cholesky(gram_full)

    def invert_one(factor_one):
        return jax.scipy.linalg.solve_triangular(factor_one, identity, lower=True)

    return jax.vmap(invert_one)(factor)


def per_device(a_left, a_right, a_rank, b_left, b_right, b_rank, c_rank, probes):
    tile_size = a_left.shape[2]
    rank_max = a_left.shape[3]
    columns = b_left.shape[1]
    probe_width = probes.shape[1]
    left_a = a_left[0]
    right_a = a_right[0]
    rank_lane = jnp.arange(rank_max)
    keep_left = (rank_lane[None, :] < a_rank[0][:, None]).astype(jnp.float32)
    keep_right = (rank_lane[None, None, :] < b_rank[:, :, None]).astype(jnp.float32)
    full_left, full_right = (
        lax.all_gather(b_left, "row", axis=2, tiled=True),
        lax.all_gather(b_right, "row", axis=2, tiled=True),
    )
    core_block = jnp.einsum(
        "knr,kjns->kjrs", right_a, full_left, preferred_element_type=jnp.float32
    )
    probed = jnp.einsum("kjnr,np->kjrp", full_right, probes, preferred_element_type=jnp.float32)
    core_block = core_block * keep_left[:, None, :, None] * keep_right[:, :, None, :]
    small_core = jnp.einsum(
        "kjrs,kjsp->kjrp", core_block, probed, precision=lax.Precision.HIGHEST
    ).astype(jnp.bfloat16)
    sketch = jnp.einsum("knr,kjrp->njp", left_a, small_core, preferred_element_type=jnp.float32)
    stacked = sketch.reshape(tile_size, columns * probe_width)
    keep_cols = (jnp.arange(probe_width)[None, :] < c_rank[0][:, None]).astype(jnp.float32)
    row_count = tile_size // lax.axis_size("inner")
    my_rows = lax.psum_scatter(stacked, "inner", scatter_dimension=0, tiled=True)
    my_cols = my_rows.reshape(row_count, columns, probe_width)
    gram_local = jnp.einsum("mcp,mcq->cpq", my_cols, my_cols, precision=lax.Precision.HIGHEST)
    gram_full = lax.psum(gram_local, "inner")
    inverse = cholesky_inverse(gram_full)
    own_basis = jnp.einsum("mcq,cpq->mcp", my_cols, inverse, precision=lax.Precision.HIGHEST)
    own_basis = (own_basis * keep_cols[None]).reshape(row_count, columns * probe_width)
    full_basis = lax.all_gather(own_basis.astype(jnp.bfloat16), "inner", axis=0, tiled=True)
    basis_out = (jnp.sqrt(jnp.float32(tile_size)) * own_basis).astype(jnp.bfloat16)[None]
    qround = full_basis.reshape(tile_size, columns, probe_width)
    projected = jnp.einsum("njp,knr->kjpr", qround, left_a, preferred_element_type=jnp.float32)
    lifted = jnp.einsum(
        "kjpr,kjrs->kjps", projected, core_block, precision=lax.Precision.HIGHEST
    ).astype(jnp.bfloat16)
    rows_term = jnp.einsum("kjns,kjps->njp", full_right, lifted, preferred_element_type=jnp.float32)
    output_rows = lax.psum_scatter(
        rows_term.reshape(tile_size, columns * probe_width).astype(jnp.bfloat16),
        "inner",
        scatter_dimension=0,
        tiled=True,
    )
    return (basis_out, output_rows[None])


def solution(mesh):
    return jax.shard_map(
        per_device,
        mesh=mesh,
        in_specs=(
            P("row", "inner", None, None),
            P("row", "inner", None, None),
            P("row", "inner"),
            P("inner", None, "row", None),
            P("inner", None, "row", None),
            P("inner", None),
            P("row", None),
            P(),
        ),
        out_specs=(P("row", "inner", None), P("row", "inner", None)),
        check_vma=False,
    )
```

profile of v0, /device:TPU:2, one launch (start us, length us, event | category | flops | bytes accessed | tf_op | source)
XLA Modules:
  0.0 636.7 jit_solution(6287523312634962393)
XLA Ops:
  8.0 0.7 all-gather.4.cloned.1.call-update
  8.7 0.7 fusion.26
  9.4 0.8 fusion.25
  10.2 77.9 %all-gather.6.cloned.1.call-done = bf16[4,4,1024,128]{3,2,1,0:T(8,128)(2,1)} async-done(((bf16[4,4,32,128]{3,2,1,0:T(8,128)(2,1)}), bf16[4,4,1024,128]{3,2,1,0:T(8,128)(2,1)}) %all-gather.6.cloned.1.call-update) | async-done | bytes 4194320 | tf_op jit(solution)/shard_map/all_gather | solution.py:31
  88.1 3.5 fusion
  91.6 69.1 %all-gather.4.cloned.1.call-done = bf16[4,4,1024,128]{3,2,1,0:T(8,128)(2,1)} async-done(((bf16[4,4,32,128]{3,2,1,0:T(8,128)(2,1)}), bf16[4,4,1024,128]{3,2,1,0:T(8,128)(2,1)}) %all-gather.4.cloned.1.call-update) | async-done | bytes 4194320 | tf_op jit(solution)/shard_map/all_gather | solution.py:30
  160.7 4.1 fusion.6
  164.8 1.8 convolution_convert_fusion.1
  166.7 2.1 fusion.9
  168.7 3.0 copy.31
  171.8 87.1 %reduce-scatter.3.cloned.1.call-done = f32[64,512]{1,0:T(8,128)} async-done(((f32[1024,512]{1,0:T(8,128)}), f32[64,512]{1,0:T(8,128)}) %reduce-scatter.3.cloned.1.call-update) | async-done | bytes 131088 | tf_op jit(solution)/shard_map/reduce_scatter | solution.py:45
  259.0 2.3 fusion.18
  261.7 115.4 %all-reduce.2.cloned.1.call-done = f32[4,128,128]{1,2,0:T(8,128)} async-done(((f32[4,128,128]{1,2,0:T(8,128)}), f32[4,128,128]{1,2,0:T(8,128)}) %all-reduce.2.cloned.1.call-update) | async-done | bytes 262160 | tf_op jit(solution)/shard_map/psum | solution.py:48
  377.1 8.5 %copy.35 = f32[4,128,128]{0,2,1:T(8,128)} copy(f32[4,128,128]{1,2,0:T(8,128)} %all-reduce.2.cloned.1.call-done) | data formatting | bytes 524288 | tf_op jit(solution)/shard_map/psum | solution.py:48
  385.6 1.8 gather_fusion
  387.7 46.9 %custom-call.8 = f32[4,128,128]{2,1,0:T(8,128)S(1)} custom-call(f32[4,128,128]{2,1,0:T(8,128)S(1)} %fusion.15), custom_call_target="Cholesky" | custom-call | tf_op jit(solution)/shard_map/jit(cholesky)/cholesky | solution.py:11
  434.9 39.3 %custom-call.9 = f32[4,1,128,128]{2,3,1,0:T(8,128)S(1)} custom-call(f32[4,1,128,128]{3,2,1,0:T(8,128)S(1)} %select_bitcast_fusion), custom_call_target="InvertDiagBlocksLowerTriangular" | custom-call | tf_op jit(solution)/shard_map/vmap(jit(_solve_triangular))/triangular_solve | solution.py:14
  476.4 57.2 %all-gather.8.cloned.1.call-done = bf16[1024,512]{1,0:T(8,128)(2,1)} async-done(((bf16[64,512]{1,0:T(8,128)(2,1)}), bf16[1024,512]{1,0:T(8,128)(2,1)}) %all-gather.8.cloned.1.call-update) | async-done | bytes 1048592 | tf_op jit(solution)/shard_map/all_gather | solution.py:52
  533.5 1.5 copy.43
  535.0 0.7 convolution_bitcast_fusion
  535.7 2.3 convolution_convert_fusion
  538.1 1.5 bitcast_convert_fusion
  539.5 1.3 copy.46
  541.6 88.2 %reduce-scatter.5.cloned.1.call-done = bf16[64,512]{1,0:T(8,128)(2,1)} async-done(((bf16[1024,512]{1,0:T(8,128)(2,1)}), bf16[64,512]{1,0:T(8,128)(2,1)}) %reduce-scatter.5.cloned.1.call-update) | async-done | bytes 65552 | tf_op jit(solution)/shard_map/reduce_scatter | solution.py:60
  (40 shorter events, 4.8 us)
Async XLA Ops:
  7.2 159.5 %copy-start = (bf16[1,4,1024,128]{3,2,1,0:T(8,128)(2,1)S(1)}, bf16[1,4,1024,128]{3,2,1,0:T(8,128)(2,1)}, u32[]{:S(2)}) copy-start(bf16[1,4,1024,128]{3,2,1,0:T(8,128)(2,1)} %param.8) | copy-start | bytes 3145732
  7.2 81.0 %all-gather.6.cloned.1.call-start = ((), (), s32[]{:S(2)}) async-start(), calls=%async_computation.3 | async-start | bytes 4325376 | tf_op jit(solution)/shard_map/all_gather | solution.py:31
  7.9 152.8 %all-gather.4.cloned.1.call-start = ((), (), s32[]{:S(2)}) async-start(), calls=%async_computation.2 | async-start | bytes 4325376 | tf_op jit(solution)/shard_map/all_gather | solution.py:30
  8.7 250.3 %reduce-scatter.3.cloned.1.call-start = ((), (), s32[]{:S(2)}) async-start(), calls=%async_computation.4 | async-start | bytes 2228224 | tf_op jit(solution)/shard_map/reduce_scatter | solution.py:45
  168.7 92.8 %copy-start.3 = (s32[1,4]{1,0:T(1,128)S(1)}, s32[1,4]{1,0:T(1,128)}, u32[]{:S(2)}) copy-start(s32[1,4]{1,0:T(1,128)} %param.14) | copy-start | bytes 52
  171.7 205.4 %all-reduce.2.cloned.1.call-start = ((), (), s32[]{:S(2)}) async-start(), calls=%async_computation.5 | async-start | bytes 524288 | tf_op jit(solution)/shard_map/psum | solution.py:48
  261.2 272.3 %all-gather.8.cloned.1.call-start = ((), (), s32[]{:S(2)}) async-start(), calls=%async_computation.6 | async-start | bytes 1114112 | tf_op jit(solution)/shard_map/all_gather | solution.py:52
  261.7 213.1 %copy-start.2 = (f32[64,512]{1,0:T(8,128)S(1)}, f32[64,512]{1,0:T(8,128)}, u32[]{:S(2)}) copy-start(f32[64,512]{1,0:T(8,128)} %reduce-scatter.3.cloned.1.call-done) | copy-start | bytes 393220
  377.1 10.3 %copy-start.1 = (f32[4,128,128]{1,2,0:T(8,128)S(1)}, f32[4,128,128]{1,2,0:T(8,128)}, u32[]{:S(2)}) copy-start(f32[4,128,128]{1,2,0:T(8,128)} %all-reduce.2.cloned.1.call-done) | copy-start | bytes 786436
  476.1 153.7 %reduce-scatter.5.cloned.1.call-start = ((), (), s32[]{:S(2)}) async-start(), calls=%async_computation.7 | async-start | bytes 1114112 | tf_op jit(solution)/shard_map/reduce_scatter | solution.py:60
  535.0 3.0 copy-start.4
Sparse Core Ops, SparseCore 0:
  10.1 77.9 all-gather.5
  90.3 70.4 all-gather.3
  171.8 87.0 reduce-scatter.2
  262.0 115.0 all-reduce.1
  476.2 57.2 all-gather.7
  541.0 88.7 reduce-scatter.4
where the time goes:
time: 637 us
  waiting for transfers between devices  496 us (78%)
  other arithmetic  88.3 us (14%)
  matrix products  19.5 us (3%)
  local copies, waits for them, and re-layouts  17.6 us (3%)
  between operations  14.3 us (2%)
    psum x1, waiting for transfers between devices, per_device(): gram_full = lax.psum(gram_local, 'inner')  115 us
    reduce_scatter x1, waiting for transfers between devices, per_device(): lax.psum_scatter(rows_term.reshape(tile_size, columns * probe_width).asty...  88.2 us
    reduce_scatter x1, waiting for transfers between devices, per_device(): lax.psum_scatter(stacked, 'inner', scatter_dimension=0, tiled=True)  87.1 us
    all_gather x1, waiting for transfers between devices, per_device(): lax.all_gather(b_right, 'row', axis=2, tiled=True)  77.9 us
    all_gather x1, waiting for transfers between devices, per_device(): lax.all_gather(b_left, 'row', axis=2, tiled=True)  69.1 us
    all_gather x1, waiting for transfers between devices, per_device(): lax.all_gather(own_basis.astype(jnp.bfloat16), 'inner', axis=0, tiled=True)  57.2 us
    another operation x4, other arithmetic, cholesky_inverse(): factor = jnp.linalg.cholesky(gram_full)  47.1 us
    another operation x3, other arithmetic, invert_one(): return jax.scipy.linalg.solve_triangular(factor_one, identity, lower=True)  39.4 us
  transfers between devices with their start and end apart: 6, of which 6 were waited for; matrix products, arithmetic and copies ran while one was open for 1% of the time, Pallas kernels for 0%

commit v1 on v0

v1 whole, which is shorter than its diff:
```python
import functools

import jax
import jax.numpy as jnp
from jax import lax
from jax.experimental import pallas as pl
from jax.experimental.pallas import tpu as pltpu
from jax.sharding import PartitionSpec as P

MESH = pl.DeviceIdType.MESH
HIGH = lax.Precision.HIGHEST
F32 = jnp.float32
BF16 = jnp.bfloat16
SUB = 8
BLOCK = 32


def dot(a, b, dims=((1,), (0,)), precision=None):
    return lax.dot_general(
        a, b, (dims, ((), ())), precision=precision, preferred_element_type=F32
    )


def factor(work):
    size = work.shape[0]
    row_of = lax.broadcasted_iota(jnp.int32, (SUB, size), 0)
    for base in range(0, size, BLOCK):
        tiles = BLOCK // SUB
        left = [work[base + SUB * t : base + SUB * (t + 1), 0:size] for t in range(tiles)]
        right = [work[base + SUB * t : base + SUB * (t + 1), size : 2 * size] for t in range(tiles)]
        for b in range(tiles):
            start = base + SUB * b
            cols = [
                [
                    jnp.broadcast_to(left[t][:, start + j : start + j + 1], (SUB, size))
                    for j in range(SUB)
                ]
                for t in range(b, tiles)
            ]
            scale = jnp.ones((SUB, size), F32)
            for i in range(SUB):
                pivot = jnp.broadcast_to(cols[0][i][i : i + 1, :], (SUB, size))
                root = lax.rsqrt(pivot)
                inv = root * root
                scale = jnp.where(row_of == i, root, scale)
                row_l = jnp.broadcast_to(left[b][i : i + 1, :], (SUB, size))
                row_r = jnp.broadcast_to(right[b][i : i + 1, :], (SUB, size))
                row_c = [
                    jnp.broadcast_to(cols[0][j][i : i + 1, :], (SUB, size))
                    for j in range(i + 1, SUB)
                ]
                for t in range(b, tiles):
                    g = cols[t - b][i] * inv
                    if t == b:
                        g = jnp.where(row_of > i, g, 0.0)
                    left[t] = left[t] - g * row_l
                    right[t] = right[t] - g * row_r
                    for j in range(i + 1, SUB):
                        cols[t - b][j] = cols[t - b][j] - g * row_c[j - i - 1]
            left[b] = left[b] * scale
            right[b] = right[b] * scale
        for t in range(tiles):
            work[base + SUB * t : base + SUB * (t + 1), 0:size] = left[t]
            work[base + SUB * t : base + SUB * (t + 1), size : 2 * size] = right[t]
        rest = base + BLOCK
        if rest < size:
            rows = jnp.concatenate(
                [jnp.concatenate(left, axis=0), jnp.concatenate(right, axis=0)], axis=1
            )
            upper = jnp.concatenate(left, axis=0)
            turned = upper.T[rest:, :]
            work[rest:, :] = work[rest:, :] - dot(turned, rows, precision=HIGH)


def kernel(
    Z, X, Y,
    a_rank, b_rank, c_rank, al_hbm, ar_hbm, bl_hbm, br_hbm, pr_hbm,
    q_out, w_out,
    BL, BR, AL, AR, PR, ART, ALT, PT, CO, CT, SM, SB, RB, ROWS, GS, GR, WK, QB, PJ, LT, CB, WB,
    in_sem, zs, zr, ps, pr, rs, rr, gs, gr, qs, qr, ws, wr,
):
    KD, COLS, NB, R = BL.shape
    PW = PT.shape[0]
    shard = bl_hbm.shape[2]
    part = NB // X
    small_part = NB // (X * Y)
    pairs = COLS // 2
    r, q = lax.axis_index("row"), lax.axis_index("inner")
    z, c = r // 2, lax.rem(r, 2)
    x, y = q // Y, lax.rem(q, Y)
    up, down = lax.rem(z + 1, Z) * 2 + c, lax.rem(z + Z - 1, Z) * 2 + c
    mate = z * 2 + 1 - c
    peers = [(dx, dy) for dx in range(X) for dy in range(Y) if dx or dy]

    def peer(dx, dy):
        return lax.rem(x + dx, X), lax.rem(y + dy, Y)

    barrier = pltpu.get_barrier_semaphore()
    ring_peers = [up, down] if Z > 2 else [up]
    for other in ring_peers + [mate]:
        pl.semaphore_signal(barrier, 1, device_id={"row": other, "inner": q}, device_id_type=MESH)
    for dx, dy in peers:
        px, py = peer(dx, dy)
        pl.semaphore_signal(barrier, 1, device_id={"row": r, "inner": px * Y + py}, device_id_type=MESH)

    mine = pl.ds(pl.multiple_of(r * shard, shard), shard)
    loads = [
        pltpu.make_async_copy(bl_hbm, BL.at[:, :, mine, :], in_sem.at[0]),
        pltpu.make_async_copy(br_hbm, BR.at[:, :, mine, :], in_sem.at[1]),
        pltpu.make_async_copy(ar_hbm.at[0], AR, in_sem.at[2]),
        pltpu.make_async_copy(al_hbm.at[0], AL, in_sem.at[3]),
        pltpu.make_async_copy(pr_hbm, PR, in_sem.at[4]),
    ]
    for load in loads:
        load.start()
    pl.semaphore_wait(barrier, len(ring_peers) + 1 + len(peers))
    loads[0].wait()
    loads[1].wait()

    tensors = (BL, BR)
    long_steps, short_steps = Z // 2, (Z - 1) // 2
    steps = ((long_steps, short_steps), (short_steps, long_steps))

    def rows_of(origin, core):
        return pl.ds(pl.multiple_of((origin * 2 + core) * shard, shard), shard)

    def ring_copy(t, d, s, origin):
        ref = tensors[t].at[:, :, rows_of(origin, c), :]
        return pltpu.make_async_remote_copy(
            ref, ref, zs.at[t, d, s], zr.at[t, d, s],
            device_id={"row": down if d else up, "inner": q}, device_id_type=MESH,
        )

    def mate_copy(t, origin, core):
        ref = tensors[t].at[:, :, rows_of(origin, core), :]
        return pltpu.make_async_remote_copy(
            ref, ref, ps.at[t, origin], pr.at[t, origin],
            device_id={"row": mate, "inner": q}, device_id_type=MESH,
        )

    def sent_origin(d, s):
        return lax.rem(z + s, Z) if d else lax.rem(z + Z - s, Z)

    for t in range(2):
        for d in range(2):
            if steps[t][d]:
                ring_copy(t, d, 0, z).start()
    for t in range(2):
        mate_copy(t, z, c).start()

    loads[2].wait()
    loads[3].wait()
    loads[4].wait()

    def turn(k):
        at = pl.ds(pl.multiple_of(k * R, R), R)
        ART[at, :] = AR[k].T
        ALT[at, :] = AL[k].T

    def hop(s, forward):
        for t in range(2):
            for d in range(2):
                if isinstance(s, int) and s >= steps[t][d]:
                    continue
                origin = sent_origin(d, s + 1)
                ring_copy(t, d, s, origin).wait_recv()
                if forward or (isinstance(s, int) and s + 1 < steps[t][d]):
                    ring_copy(t, d, s + 1, origin).start()
                mate_copy(t, origin, c).start()

    def hop_loop(s, carry):
        hop(s, True)

        @pl.when(s < KD)
        def _():
            turn(s)

        return carry

    uniform = max(short_steps - 1, 0)
    lax.fori_loop(0, uniform, hop_loop, 0)
    for k in range(min(uniform, KD), KD):
        turn(k)
    PT[...] = PR[...].T
    for s in range(uniform, long_steps):
        hop(s, False)

    def mate_wait(t):
        def body(o, carry):
            mate_copy(t, o, 1 - c).wait_recv()
            return carry

        lax.fori_loop(0, Z, body, 0)

    mate_wait(0)
    mate_wait(1)

    row_lane = lax.broadcasted_iota(jnp.int32, (R, R), 0)
    col_lane = lax.broadcasted_iota(jnp.int32, (R, R), 1)

    def cores(k, carry):
        at = pl.ds(pl.multiple_of(k * R, R), R)
        lhs = ART[at, :]
        for g in range(pairs):
            j0 = 2 * g
            both = dot(lhs, jnp.concatenate([BL[k, j0], BL[k, j0 + 1]], axis=1))
            probed = dot(PT[...], jnp.concatenate([BR[k, j0], BR[k, j0 + 1]], axis=1))
            for h in range(2):
                j = j0 + h
                keep = jnp.logical_and(row_lane < a_rank[0, k], col_lane < b_rank[k, j])
                core = jnp.where(keep, both[:, h * R : (h + 1) * R], 0.0)
                CO[k, j] = core
                small = dot(core, probed[:, h * R : (h + 1) * R], ((1,), (1,)), HIGH)
                SM[at, j * PW : (j + 1) * PW] = small.astype(BF16)
        return carry

    lax.fori_loop(0, KD, cores, 0)

    def sketch_rows(px):
        at = pl.ds(pl.multiple_of(px * part, part), part)
        lhs = jnp.concatenate([AL[k, at, :] for k in range(KD)], axis=1)
        rows = dot(lhs, SM[...])
        for j in range(COLS):
            SB[px * Y + j] = rows[:, j * PW : (j + 1) * PW].astype(BF16)

    def block_copy(src, dst, send, recv, e, target):
        return pltpu.make_async_remote_copy(
            src.at[target], dst.at[e], send.at[e], recv.at[e],
            device_id={"row": r, "inner": target}, device_id_type=MESH,
        )

    def send_column(dx, src, dst, send, recv, first):
        def body(dy, carry):
            px, py = lax.rem(x + dx, X), lax.rem(y + dy, Y)
            block_copy(src, dst, send, recv, dx * Y + dy, px * Y + py).start()
            return carry

        lax.fori_loop(first, Y, body, 0)

    def sketch_loop(dx, carry):
        sketch_rows(lax.rem(x + dx, X))
        send_column(dx, SB, RB, rs, rr, 0)
        return carry

    lax.fori_loop(1, X, sketch_loop, 0)
    sketch_rows(x)
    send_column(0, SB, RB, rs, rr, 1)

    def turn_cores(k, carry):
        for j in range(COLS):
            CT[k, j] = CO[k, j].T
        return carry

    lax.fori_loop(0, KD, turn_cores, 0)

    def gather_sum(src, dst, send, recv):
        total = src[q].astype(F32)
        for e in range(1, X * Y):
            block_copy(src, dst, send, recv, e, q).wait_recv()
            total = total + dst[e].astype(F32)
        return total

    ROWS[...] = gather_sum(SB, RB, rs, rr)

    own_rows = ROWS[...]
    GS[...] = dot(own_rows.T, own_rows, precision=HIGH)

    def gram_copy(dx):
        px = lax.rem(x + dx, X)
        return pltpu.make_async_remote_copy(
            GS, GR.at[dx], gs.at[dx], gr.at[dx],
            device_id={"row": r, "inner": px * Y + y}, device_id_type=MESH,
        )

    for dx in range(1, X):
        gram_copy(dx).start()
    gram = GS[...]
    for dx in range(1, X):
        gram_copy(dx).wait_recv()
        gram = gram + GR[dx]
    eye = row_lane == col_lane
    mean = jnp.sum(jnp.where(eye, gram, 0.0), keepdims=True) / PW
    gram = gram + jnp.where(eye, 0.0001 * mean, 0.0)
    WK[:, 0:PW] = gram
    WK[:, PW : 2 * PW] = jnp.where(eye, 1.0, 0.0)
    factor(WK)
    basis = dot(ROWS[...], WK[:, PW : 2 * PW], ((1,), (1,)), HIGH)
    lane = lax.broadcasted_iota(jnp.int32, basis.shape, 1)
    basis = jnp.where(lane < c_rank[0, y], basis, 0.0)
    own_at = pl.ds(pl.multiple_of(x * part, part), part)
    QB[y, own_at, :] = basis.astype(BF16)

    def basis_copy(e, sx, sy, px, py):
        ref = QB.at[sy, pl.ds(pl.multiple_of(sx * part, part), part), :]
        return pltpu.make_async_remote_copy(
            ref, ref, qs.at[e], qr.at[e],
            device_id={"row": r, "inner": px * Y + py}, device_id_type=MESH,
        )

    for dx, dy in peers:
        px, py = peer(dx, dy)
        basis_copy(dx * Y + dy, x, y, px, py).start()
    for dx, dy in peers:
        sx, sy = lax.rem(x + X - dx, X), lax.rem(y + Y - dy, Y)
        basis_copy(dx * Y + dy, sx, sy, x, y).wait_recv()

    out_at = pl.ds(pl.multiple_of(q * small_part, small_part), small_part)
    for j in range(COLS):
        q_out[0, :, j * PW : (j + 1) * PW] = (
            jnp.sqrt(jnp.float32(NB)) * QB[j, out_at, :].astype(F32)
        ).astype(BF16)

    for g in range(pairs):
        PJ[:, 2 * g * PW : (2 * g + 2) * PW] = dot(
            ALT[...], jnp.concatenate([QB[2 * g], QB[2 * g + 1]], axis=1)
        )

    def lift(k, carry):
        at = pl.ds(pl.multiple_of(k * R, R), R)
        for j in range(COLS):
            lifted = dot(CT[k, j], PJ[at, j * PW : (j + 1) * PW], precision=HIGH)
            LT[at, j * PW : (j + 1) * PW] = lifted.astype(BF16)
        return carry

    lax.fori_loop(0, KD, lift, 0)

    def coeff_rows(px):
        at = pl.ds(pl.multiple_of(px * part, part), part)
        for j in range(COLS):
            lhs = jnp.concatenate([BR[k, j, at, :] for k in range(KD)], axis=1)
            rows = dot(lhs, LT[:, j * PW : (j + 1) * PW]).astype(BF16)
            for h in range(Y):
                CB[px * Y + h, :, j * PW : (j + 1) * PW] = rows[h * small_part : (h + 1) * small_part, :]

    def coeff_loop(dx, carry):
        coeff_rows(lax.rem(x + dx, X))
        send_column(dx, CB, WB, ws, wr, 0)
        return carry

    lax.fori_loop(1, X, coeff_loop, 0)
    coeff_rows(x)
    send_column(0, CB, WB, ws, wr, 1)
    w_out[0] = gather_sum(CB, WB, ws, wr).astype(BF16)

    for t in range(2):
        for d in range(2):
            for s in range(steps[t][d]):
                ring_copy(t, d, s, z).wait_send()

        def sent(o, carry):
            mate_copy(t, o, c).wait_send()
            return carry

        lax.fori_loop(0, Z, sent, 0)
    for e in range(1, X * Y):
        block_copy(SB, RB, rs, rr, e, q).wait_send()
        basis_copy(e, x, y, x, y).wait_send()
        block_copy(CB, WB, ws, wr, e, q).wait_send()
    for dx in range(1, X):
        gram_copy(dx).wait_send()


def per_device(Z, X, Y, a_left, a_right, a_rank, b_left, b_right, b_rank, c_rank, probes):
    _, KD, NB, R = a_left.shape
    COLS = b_left.shape[1]
    PW = probes.shape[1]
    part, small_part = NB // X, NB // (X * Y)
    n = X * Y
    long_steps = max(Z // 2, 1)
    any_space = pl.BlockSpec(memory_space=pl.ANY)
    smem = pl.BlockSpec(memory_space=pltpu.SMEM)
    vmem = pl.BlockSpec(memory_space=pltpu.VMEM)
    dma = pltpu.SemaphoreType.DMA
    V = pltpu.VMEM
    out = jax.ShapeDtypeStruct((1, small_part, COLS * PW), BF16)
    return pl.pallas_call(
        functools.partial(kernel, Z, X, Y),
        out_shape=(out, out),
        in_specs=[smem] * 3 + [any_space] * 5,
        out_specs=(vmem, vmem),
        scratch_shapes=[
            V((KD, COLS, NB, R), BF16),
            V((KD, COLS, NB, R), BF16),
            V((KD, NB, R), BF16),
            V((KD, NB, R), BF16),
            V((NB, PW), BF16),
            V((KD * R, NB), BF16),
            V((KD * R, NB), BF16),
            V((PW, NB), BF16),
            V((KD, COLS, R, R), F32),
            V((KD, COLS, R, R), F32),
            V((KD * R, COLS * PW), BF16),
            V((n, part, PW), BF16),
            V((n, part, PW), BF16),
            V((part, PW), F32),
            V((PW, PW), F32),
            V((X, PW, PW), F32),
            V((PW, 2 * PW), F32),
            V((COLS, NB, PW), BF16),
            V((KD * R, COLS * PW), F32),
            V((KD * R, COLS * PW), BF16),
            V((n, small_part, COLS * PW), BF16),
            V((n, small_part, COLS * PW), BF16),
            dma((5,)),
            dma((2, 2, long_steps)), dma((2, 2, long_steps)),
            dma((2, Z)), dma((2, Z)),
            dma((n,)), dma((n,)),
            dma((X,)), dma((X,)),
            dma((n,)), dma((n,)),
            dma((n,)), dma((n,)),
        ],
        compiler_params=pltpu.CompilerParams(collective_id=0, has_side_effects=True),
    )(a_rank, b_rank, c_rank, a_left, a_right, b_left, b_right, probes)


def solution(mesh):
    Z = mesh.shape["row"] // 2
    Y = 4
    X = mesh.shape["inner"] // Y
    return jax.shard_map(
        functools.partial(per_device, Z, X, Y),
        mesh=mesh,
        in_specs=(
            P("row", "inner", None, None),
            P("row", "inner", None, None),
            P("row", "inner"),
            P("inner", None, "row", None),
            P("inner", None, "row", None),
            P("inner", None),
            P("row", None),
            P(),
        ),
        out_specs=(P("row", "inner", None), P("row", "inner", None)),
        check_vma=False,
    )
```

time: 637 us -> 132 us (0.21)
  the two profiles are of different devices: /device:TPU:2 before, /device:TPU:8 now
where the time goes in v1:
time: 132 us
  Pallas kernels  129 us (98%)
  local copies, waits for them, and re-layouts  2.14 us (2%)
    pallas_call x1, Pallas kernels, per_device(): pl.pallas_call(functools.partial(kernel, Z, X, Y), out_shape=(out, out),...  129 us

profile of v1, /device:TPU:8, one launch (start us, length us, event | category | flops | bytes accessed | tf_op | source)
XLA Modules:
  0.0 132.1 jit_solution(8535701666427419668)
XLA Ops:
  0.6 129.3 %shard_map.95 = (bf16[1,64,512]{2,1,0:T(8,128)(2,1)}, bf16[1,64,512]{2,1,0:T(8,128)(2,1)}) custom-call(s32[1,4]{1,0:T(1,128)} %a_rank.1, s32[4,4]{1,0:T(4,128)} %b_rank.1, s32[1,4]{1,0:T(1,128)} %c_rank.1, bf16[1,4,1024,128]{3,2,1,0:T(8,128)(2,1)} %al_hbm.1, bf16[1,4,1024,128]{3,2,1,0:T(8,128)(2,1)} %ar_hbm.1, bf16[4,4,32,128]{3,2,1,0:T(8,128)(2,1)} %bl_hbm.1, ...), custom_call_target="tpu_custom_call" | custom-call | tf_op jit(solution)/shard_map/pallas_call | solution.py:376
  129.9 0.0 copy-start
  130.0 1.5 %copy.12 = bf16[1,64,512]{2,1,0:T(8,128)(2,1)} copy(bf16[1,64,512]{2,1,0:T(8,128)(2,1)} %get-tuple-element.4) | data formatting | bytes 131072
  131.5 0.0 copy-done
  131.5 0.6 copy.13
Async XLA Ops:
  129.9 1.5 %copy-start = (bf16[1,64,512]{2,1,0:T(8,128)(2,1)S(1)}, bf16[1,64,512]{2,1,0:T(8,128)(2,1)}, u32[]{:S(2)}) copy-start(bf16[1,64,512]{2,1,0:T(8,128)(2,1)} %get-tuple-element.5) | copy-start | bytes 196612

commit v2 on v1

v2 whole, which is shorter than its diff:
```python
import functools

import jax
import jax.numpy as jnp
from jax import lax
from jax.experimental import pallas as pl
from jax.experimental.pallas import tpu as pltpu
from jax.sharding import PartitionSpec as P

MESH = pl.DeviceIdType.MESH
HIGH = lax.Precision.HIGHEST
F32 = jnp.float32
BF16 = jnp.bfloat16
SUB = 8
CHUNKS = 2
BLOCK = 32


def dot(a, b, dims=((1,), (0,)), precision=None):
    return lax.dot_general(
        a, b, (dims, ((), ())), precision=precision, preferred_element_type=F32
    )


def factor(work):
    size = work.shape[0]
    row_of = lax.broadcasted_iota(jnp.int32, (SUB, size), 0)
    for base in range(0, size, BLOCK):
        tiles = BLOCK // SUB
        left = [work[base + SUB * t : base + SUB * (t + 1), 0:size] for t in range(tiles)]
        right = [work[base + SUB * t : base + SUB * (t + 1), size : 2 * size] for t in range(tiles)]
        for b in range(tiles):
            start = base + SUB * b
            cols = [
                [
                    jnp.broadcast_to(left[t][:, start + j : start + j + 1], (SUB, size))
                    for j in range(SUB)
                ]
                for t in range(b, tiles)
            ]
            scale = jnp.ones((SUB, size), F32)
            for i in range(SUB):
                pivot = jnp.broadcast_to(cols[0][i][i : i + 1, :], (SUB, size))
                root = lax.rsqrt(pivot)
                inv = root * root
                scale = jnp.where(row_of == i, root, scale)
                row_l = jnp.broadcast_to(left[b][i : i + 1, :], (SUB, size))
                row_r = jnp.broadcast_to(right[b][i : i + 1, :], (SUB, size))
                row_c = [
                    jnp.broadcast_to(cols[0][j][i : i + 1, :], (SUB, size))
                    for j in range(i + 1, SUB)
                ]
                for t in range(b, tiles):
                    g = cols[t - b][i] * inv
                    if t == b:
                        g = jnp.where(row_of > i, g, 0.0)
                    left[t] = left[t] - g * row_l
                    right[t] = right[t] - g * row_r
                    for j in range(i + 1, SUB):
                        cols[t - b][j] = cols[t - b][j] - g * row_c[j - i - 1]
            left[b] = left[b] * scale
            right[b] = right[b] * scale
        for t in range(tiles):
            work[base + SUB * t : base + SUB * (t + 1), 0:size] = left[t]
            work[base + SUB * t : base + SUB * (t + 1), size : 2 * size] = right[t]
        rest = base + BLOCK
        if rest < size:
            rows = jnp.concatenate(
                [jnp.concatenate(left, axis=0), jnp.concatenate(right, axis=0)], axis=1
            )
            upper = jnp.concatenate(left, axis=0)
            turned = upper.T[rest:, :]
            work[rest:, :] = work[rest:, :] - dot(turned, rows, precision=HIGH)


def kernel(
    Z, X, Y,
    a_rank, b_rank, c_rank, al_hbm, ar_hbm, bl_hbm, br_hbm, pr_hbm,
    q_out, w_out,
    BL, BR, AL, AR, PR, ALT, PB, CO, CT, SM, SF, SG, ST, SU, ROWS, GS, GR, WK, NI, QB, PJ, LT, CF, CG, CT2, CU,
    in_sem, zs, zr, ps, pr, rs, rr, gs, gr, ns, nr, qs, qr,
):
    KD, COLS, NB, R = BL.shape
    PW = PR.shape[1]
    shard = bl_hbm.shape[2]
    part = NB // X
    halfpart = part // 2
    small_part = NB // (X * Y)
    pairs = COLS // 2
    r, q = lax.axis_index("row"), lax.axis_index("inner")
    z, c = r // 2, lax.rem(r, 2)
    x, y = q // Y, lax.rem(q, Y)
    up, down = lax.rem(z + 1, Z) * 2 + c, lax.rem(z + Z - 1, Z) * 2 + c
    mate = z * 2 + 1 - c
    peers = [(dx, dy) for dx in range(X) for dy in range(Y) if dx or dy]

    def peer(dx, dy):
        return lax.rem(x + dx, X), lax.rem(y + dy, Y)

    barrier = pltpu.get_barrier_semaphore()
    ring_peers = [up, down] if Z > 2 else [up]
    for other in ring_peers + [mate]:
        pl.semaphore_signal(barrier, 1, device_id={"row": other, "inner": q}, device_id_type=MESH)
    for dx, dy in peers:
        px, py = peer(dx, dy)
        pl.semaphore_signal(barrier, 1, device_id={"row": r, "inner": px * Y + py}, device_id_type=MESH)

    mine = pl.ds(pl.multiple_of(r * shard, shard), shard)
    loads = [
        pltpu.make_async_copy(bl_hbm, BL.at[:, :, mine, :], in_sem.at[0]),
        pltpu.make_async_copy(br_hbm, BR.at[:, :, mine, :], in_sem.at[1]),
        pltpu.make_async_copy(ar_hbm.at[0], AR, in_sem.at[2]),
        pltpu.make_async_copy(al_hbm.at[0], AL, in_sem.at[3]),
        pltpu.make_async_copy(pr_hbm, PR, in_sem.at[4]),
    ]
    for load in loads:
        load.start()
    pl.semaphore_wait(barrier, len(ring_peers) + 1 + len(peers))

    tensors, given = (BL, BR), (bl_hbm, br_hbm)
    long_steps, short_steps = Z // 2, (Z - 1) // 2
    steps = ((long_steps, short_steps), (short_steps, long_steps))

    def rows_of(origin, core):
        return pl.ds(pl.multiple_of((origin * 2 + core) * shard, shard), shard)

    half = KD // CHUNKS

    def ring_copy(t, h, d, s, origin, own=False):
        ref = tensors[t].at[h * half : (h + 1) * half, :, rows_of(origin, c), :]
        src = given[t].at[h * half : (h + 1) * half] if own else ref
        return pltpu.make_async_remote_copy(
            src, ref, zs.at[t, h, d, s], zr.at[t, h, d, s],
            device_id={"row": down if d else up, "inner": q}, device_id_type=MESH,
        )

    def mate_copy(t, h, origin, core, own=False):
        ref = tensors[t].at[h * half : (h + 1) * half, :, rows_of(origin, core), :]
        src = given[t].at[h * half : (h + 1) * half] if own else ref
        return pltpu.make_async_remote_copy(
            src, ref, ps.at[t, h, origin], pr.at[t, h, origin],
            device_id={"row": mate, "inner": q}, device_id_type=MESH,
        )

    def sent_origin(d, s):
        return lax.rem(z + s, Z) if d else lax.rem(z + Z - s, Z)

    chunks = [(t, h) for t in range(2) for h in range(CHUNKS)]
    for t, h in chunks:
        for d in range(2):
            if steps[t][d]:
                ring_copy(t, h, d, 0, z, True).start()
    for t, h in chunks:
        mate_copy(t, h, z, c, True).start()

    loads[0].wait()
    loads[1].wait()
    loads[2].wait()
    loads[3].wait()
    loads[4].wait()
    CO[...] = jnp.zeros(CO.shape, F32)
    PB[...] = jnp.zeros(PB.shape, F32)

    def turn(k):
        at = pl.ds(pl.multiple_of(k * R, R), R)
        ALT[at, :] = AL[k].T

    def mate_wait(origins):
        for o in origins:
            for t, h in chunks:
                mate_copy(t, h, o, 1 - c).wait_recv()

    def absorb(origins):
        ats = [pl.ds(pl.multiple_of(o * 2 * shard, 2 * shard), 2 * shard) for o in origins]

        def stack(parts):
            return jnp.concatenate(parts, axis=0) if len(parts) > 1 else parts[0]

        probe = stack([PR[at, :] for at in ats]).T

        def body(k, carry):
            lhs = stack([AR[k, at, :] for at in ats]).T
            for g in range(pairs):
                for ref, left, total in ((BL, lhs, CO), (BR, probe, PB)):
                    rhs = jnp.concatenate(
                        [stack([ref[k, 2 * g + h, at, :] for at in ats]) for h in range(2)], axis=1
                    )
                    total[k, g] += dot(left, rhs)
            return carry

        lax.fori_loop(0, KD, body, 0)

    def hop(s, forward):
        for t, h in chunks:
            for d in range(2):
                if isinstance(s, int) and s >= steps[t][d]:
                    continue
                origin = sent_origin(d, s + 1)
                ring_copy(t, h, d, s, origin).wait_recv()
                if forward or (isinstance(s, int) and s + 1 < steps[t][d]):
                    ring_copy(t, h, d, s + 1, origin).start()
                mate_copy(t, h, origin, c).start()

    def both(s):
        return sent_origin(0, s), sent_origin(1, s)

    uniform = max(short_steps - 1, 0)
    if uniform:
        hop(0, True)
        mate_wait([z])
        absorb([z])

        def hop_loop(s, carry):
            hop(s, True)

            @pl.when(s < KD + 1)
            def _():
                turn(s - 1)

            mate_wait(both(s))
            absorb(both(s))
            return carry

        lax.fori_loop(1, uniform, hop_loop, 0)
        for k in range(min(uniform - 1, KD), KD):
            turn(k)
        done = uniform
    else:
        for k in range(KD):
            turn(k)
        mate_wait([z])
        absorb([z])
        done = 1
    for s in range(uniform, long_steps):
        hop(s, False)
        if 1 <= s:
            mate_wait(both(s))
            absorb(both(s))
    if Z > 1:
        last = [sent_origin(0, long_steps)]
        if short_steps == long_steps:
            last.append(sent_origin(1, long_steps))
        mate_wait(last)
        absorb(last)

    row_lane = lax.broadcasted_iota(jnp.int32, (R, R), 0)
    col_lane = lax.broadcasted_iota(jnp.int32, (R, R), 1)

    def cores(k, carry):
        at = pl.ds(pl.multiple_of(k * R, R), R)
        for j in range(COLS):
            g, at_j = j // 2, slice((j % 2) * R, (j % 2 + 1) * R)
            keep = jnp.logical_and(row_lane < a_rank[0, k], col_lane < b_rank[k, j])
            core = jnp.where(keep, CO[k, g, :, at_j], 0.0)
            CO[k, g, :, at_j] = core
            small = dot(core, PB[k, g, :, at_j], ((1,), (1,)), HIGH)
            SM[at, j * PW : (j + 1) * PW] = small.astype(BF16)
        return carry

    lax.fori_loop(0, KD, cores, 0)

    size, me = (X, Y), (x, y)

    def line(p, d):
        px, py = (lax.rem(x + d, X), y) if p == 0 else (x, lax.rem(y + d, Y))
        return {"row": r, "inner": px * Y + py}

    def first_copy(i, F, G, p, d):
        return pltpu.make_async_remote_copy(
            F.at[p, lax.rem(me[p] + d, size[p])], G.at[p, d], rs.at[i, 0, p, d], rr.at[i, 0, p, d],
            device_id=line(p, d), device_id_type=MESH,
        )

    def second_copy(i, T, U, p, d):
        return pltpu.make_async_remote_copy(
            T.at[p, lax.rem(me[1 - p] + d, size[1 - p])], U.at[p, d], rs.at[i, 1, p, d], rr.at[i, 1, p, d],
            device_id=line(1 - p, d), device_id_type=MESH,
        )

    def spread(i, compute, F, G):
        def body(d, carry):
            compute(lax.rem(x + d, X))
            first_copy(i, F, G, 0, d).start()
            return carry

        lax.fori_loop(1, X, body, 0)
        compute(x)
        for d in range(1, Y):
            first_copy(i, F, G, 1, d).start()

    def middle(i, F, G, T, U):
        for p in range(2):
            for d in range(1, size[p]):
                first_copy(i, F, G, p, d).wait_recv()

            def body(d, carry):
                o = lax.rem(me[1 - p] + d, size[1 - p])
                total = F[p, me[p], o].astype(F32)
                for e in range(1, size[p]):
                    total = total + G[p, e, o].astype(F32)
                T[p, o] = total.astype(BF16)
                return carry

            lax.fori_loop(1, size[1 - p] + 1, body, 0)
            for d in range(1, size[1 - p]):
                second_copy(i, T, U, p, d).start()

    def final(i, T, U, p):
        total = T[p, me[1 - p]].astype(F32)
        for d in range(1, size[1 - p]):
            second_copy(i, T, U, p, d).wait_recv()
            total = total + U[p, d].astype(F32)
        return total

    def sketch_rows(px):
        at = pl.ds(pl.multiple_of(px * part, part), part)
        lhs = jnp.concatenate([AL[k, at, :] for k in range(KD)], axis=1)
        rows = dot(lhs, SM[...]).astype(BF16)
        for j in range(COLS):
            SF[0, px, j] = rows[:halfpart, j * PW : (j + 1) * PW]
            SF[1, j, px] = rows[halfpart:, j * PW : (j + 1) * PW]

    spread(0, sketch_rows, SF, SG)

    def turn_cores(k, carry):
        for j in range(COLS):
            CT[k, j] = CO[k, j // 2, :, (j % 2) * R : (j % 2 + 1) * R].T
        return carry

    lax.fori_loop(0, KD, turn_cores, 0)

    middle(0, SF, SG, ST, SU)
    for p in range(2):
        ROWS[p * halfpart : (p + 1) * halfpart, :] = final(0, ST, SU, p)

    own_rows = ROWS[...]
    GS[...] = dot(own_rows.T, own_rows, precision=HIGH)

    def gram_copy(dx):
        px = lax.rem(x + dx, X)
        return pltpu.make_async_remote_copy(
            GS, GR.at[dx], gs.at[dx], gr.at[dx],
            device_id={"row": r, "inner": px * Y + y}, device_id_type=MESH,
        )

    for dx in range(1, X):
        gram_copy(dx).start()

    for p in range(2):
        QB[y, x, p] = own_rows[p * halfpart : (p + 1) * halfpart, :].astype(BF16)

    def share_copy(step, p, d, sx, sy):
        if step == 0:
            ref = QB.at[sy, sx, p]
        else:
            ref = QB.at[sy, :, 0] if p == 0 else QB.at[:, sx, 1]
        return pltpu.make_async_remote_copy(
            ref, ref, qs.at[step, p, d], qr.at[step, p, d],
            device_id=line(p if step == 0 else 1 - p, d), device_id_type=MESH,
        )

    def share_wait(step, p):
        along = p if step == 0 else 1 - p
        for d in range(1, size[along]):
            sx = lax.rem(x + X - d, X) if along == 0 else x
            sy = lax.rem(y + Y - d, Y) if along == 1 else y
            share_copy(step, p, d, sx, sy).wait_recv()

    def share_start(step, p):
        for d in range(1, size[p if step == 0 else 1 - p]):
            share_copy(step, p, d, x, y).start()

    share_start(0, 0)
    share_start(0, 1)
    for p in range(2):
        share_wait(0, p)
        share_start(1, p)

    gram = GS[...]
    for dx in range(1, X):
        gram_copy(dx).wait_recv()
        gram = gram + GR[dx]
    eye = row_lane == col_lane
    mean = jnp.sum(jnp.where(eye, gram, 0.0), keepdims=True) / PW
    gram = gram + jnp.where(eye, 0.0001 * mean, 0.0)
    WK[:, 0:PW] = gram
    WK[:, PW : 2 * PW] = jnp.where(eye, 1.0, 0.0)
    factor(WK)
    NI[y] = WK[:, PW : 2 * PW]

    def inverse_copy(dy, sy, py):
        return pltpu.make_async_remote_copy(
            NI.at[sy], NI.at[sy], ns.at[dy], nr.at[dy],
            device_id={"row": r, "inner": x * Y + py}, device_id_type=MESH,
        )

    for dy in range(1, Y):
        inverse_copy(dy, y, lax.rem(y + dy, Y)).start()
    for p in range(2):
        share_wait(1, p)

    for g in range(pairs):
        PJ[:, 2 * g * PW : (2 * g + 2) * PW] = dot(
            ALT[...], jnp.concatenate([QB[2 * g + h].reshape(NB, PW) for h in range(2)], axis=1)
        )
    for dy in range(1, Y):
        inverse_copy(dy, lax.rem(y + Y - dy, Y), y).wait_recv()

    def orthonormal(rows, j):
        turned = dot(rows, NI[j], ((1,), (1,)), HIGH)
        lane = lax.broadcasted_iota(jnp.int32, turned.shape, 1)
        return jnp.where(lane < c_rank[0, j], turned, 0.0)

    for j in range(COLS):
        at_j = slice(j * PW, (j + 1) * PW)
        PJ[:, at_j] = orthonormal(PJ[:, at_j], j)

    def lift(k, carry):
        at = pl.ds(pl.multiple_of(k * R, R), R)
        for j in range(COLS):
            lifted = dot(CT[k, j], PJ[at, j * PW : (j + 1) * PW], precision=HIGH)
            LT[at, j * PW : (j + 1) * PW] = lifted.astype(BF16)
        return carry

    lax.fori_loop(0, KD, lift, 0)

    def coeff_rows(px):
        at = pl.ds(pl.multiple_of(px * part, part), part)
        cut = small_part // 2
        for j in range(COLS):
            at_j = slice(j * PW, (j + 1) * PW)
            lhs = jnp.concatenate([BR[k, j, at, :] for k in range(KD)], axis=1)
            rows = dot(lhs, LT[:, at_j]).astype(BF16)
            for h in range(Y):
                CF[0, px, h, :, at_j] = rows[h * small_part : h * small_part + cut, :]
                CF[1, h, px, :, at_j] = rows[h * small_part + cut : (h + 1) * small_part, :]

    spread(1, coeff_rows, CF, CG)
    for j in range(COLS):
        at_q = pl.ds(pl.multiple_of(lax.rem(y, Y // 2) * small_part, small_part), small_part)
        own = orthonormal(QB[j, x, y // (Y // 2), at_q, :].astype(F32), j)
        q_out[:, j * PW : (j + 1) * PW] = jnp.sqrt(jnp.float32(NB)) * own
    middle(1, CF, CG, CT2, CU)
    for p in range(2):
        cut = small_part // 2
        w_out[p * cut : (p + 1) * cut, :] = final(1, CT2, CU, p)

    for t, h in chunks:
        for d in range(2):
            for s in range(steps[t][d]):
                ring_copy(t, h, d, s, z).wait_send()

        def sent(o, carry):
            mate_copy(t, h, o, c).wait_send()
            return carry

        lax.fori_loop(0, Z, sent, 0)
    for p in range(2):
        for i, (F, G, T, U) in enumerate(((SF, SG, ST, SU), (CF, CG, CT2, CU))):
            for d in range(1, size[p]):
                first_copy(i, F, G, p, d).wait_send()
            for d in range(1, size[1 - p]):
                second_copy(i, T, U, p, d).wait_send()
        for step in range(2):
            for d in range(1, size[p if step == 0 else 1 - p]):
                share_copy(step, p, d, x, y).wait_send()
    for dx in range(1, X):
        gram_copy(dx).wait_send()
    for dy in range(1, Y):
        inverse_copy(dy, y, y).wait_send()


def per_device(Z, X, Y, a_left, a_right, a_rank, b_left, b_right, b_rank, c_rank, probes):
    _, KD, NB, R = a_left.shape
    COLS = b_left.shape[1]
    PW = probes.shape[1]
    part, small_part = NB // X, NB // (X * Y)
    m, half = max(X, Y), part // 2
    long_steps = max(Z // 2, 1)
    any_space = pl.BlockSpec(memory_space=pl.ANY)
    smem = pl.BlockSpec(memory_space=pltpu.SMEM)
    vmem = pl.BlockSpec(memory_space=pltpu.VMEM)
    dma = pltpu.SemaphoreType.DMA
    V = pltpu.VMEM
    out = jax.ShapeDtypeStruct((small_part, COLS * PW), F32)
    q_basis, w_factor = pl.pallas_call(
        functools.partial(kernel, Z, X, Y),
        out_shape=(out, out),
        in_specs=[smem] * 3 + [any_space] * 5,
        out_specs=(vmem, vmem),
        scratch_shapes=[
            V((KD, COLS, NB, R), BF16),
            V((KD, COLS, NB, R), BF16),
            V((KD, NB, R), BF16),
            V((KD, NB, R), BF16),
            V((NB, PW), BF16),
            V((KD * R, NB), BF16),
            V((KD, COLS // 2, PW, 2 * R), F32),
            V((KD, COLS // 2, R, 2 * R), F32),
            V((KD, COLS, R, R), F32),
            V((KD * R, COLS * PW), BF16),
            V((2, m, m, half, PW), BF16),
            V((2, m, m, half, PW), BF16),
            V((2, m, half, PW), BF16),
            V((2, m, half, PW), BF16),
            V((part, PW), F32),
            V((PW, PW), F32),
            V((X, PW, PW), F32),
            V((PW, 2 * PW), F32),
            V((COLS, PW, PW), F32),
            V((COLS, X, 2, half, PW), BF16),
            V((KD * R, COLS * PW), F32),
            V((KD * R, COLS * PW), BF16),
            V((2, m, m, small_part // 2, COLS * PW), BF16),
            V((2, m, m, small_part // 2, COLS * PW), BF16),
            V((2, m, small_part // 2, COLS * PW), BF16),
            V((2, m, small_part // 2, COLS * PW), BF16),
            dma((5,)),
            dma((2, CHUNKS, 2, long_steps)), dma((2, CHUNKS, 2, long_steps)),
            dma((2, CHUNKS, Z)), dma((2, CHUNKS, Z)),
            dma((2, 2, 2, m)), dma((2, 2, 2, m)),
            dma((X,)), dma((X,)),
            dma((Y,)), dma((Y,)),
            dma((2, 2, m)), dma((2, 2, m)),
        ],
        compiler_params=pltpu.CompilerParams(collective_id=0, has_side_effects=True),
    )(a_rank, b_rank, c_rank, a_left, a_right, b_left, b_right, probes)
    return q_basis.astype(BF16)[None], w_factor.astype(BF16)[None]


def solution(mesh):
    Z = mesh.shape["row"] // 2
    Y = 4
    X = mesh.shape["inner"] // Y
    return jax.shard_map(
        functools.partial(per_device, Z, X, Y),
        mesh=mesh,
        in_specs=(
            P("row", "inner", None, None),
            P("row", "inner", None, None),
            P("row", "inner"),
            P("inner", None, "row", None),
            P("inner", None, "row", None),
            P("inner", None),
            P("row", None),
            P(),
        ),
        out_specs=(P("row", "inner", None), P("row", "inner", None)),
        check_vma=False,
    )
```

time: 132 us -> 116 us (0.88)
  the two profiles are of different devices: /device:TPU:8 before, /device:TPU:2 now
where the time goes in v2:
time: 116 us
  Pallas kernels  114 us (98%)
  other arithmetic  1.63 us (1%)
    pallas_call x1, Pallas kernels, per_device(): pl.pallas_call(functools.partial(kernel, Z, X, Y), out_shape=(out, out),...  114 us

profile of v2, /device:TPU:2, one launch (start us, length us, event | category | flops | bytes accessed | tf_op | source)
XLA Modules:
  0.0 116.3 jit_solution(17465578364897079801)
XLA Ops:
  0.6 114.0 %shard_map.95 = (f32[64,512]{1,0:T(8,128)}, f32[64,512]{1,0:T(8,128)}) custom-call(s32[1,4]{1,0:T(1,128)} %a_rank.1, s32[4,4]{1,0:T(4,128)} %b_rank.1, s32[1,4]{1,0:T(1,128)} %c_rank.1, bf16[1,4,1024,128]{3,2,1,0:T(8,128)(2,1)} %al_hbm.1, bf16[1,4,1024,128]{3,2,1,0:T(8,128)(2,1)} %ar_hbm.1, bf16[4,4,32,128]{3,2,1,0:T(8,128)(2,1)} %bl_hbm.1, ...), custom_call_target="tpu_custom_call" | custom-call | tf_op jit(solution)/shard_map/pallas_call | solution.py:486
  114.7 1.6 %convert_bitcast_fusion = (bf16[1,64,512]{2,1,0:T(8,128)(2,1)}, bf16[1,64,512]{2,1,0:T(8,128)(2,1)}) fusion(f32[64,512]{1,0:T(8,128)} %get-tuple-element.5, f32[64,512]{1,0:T(8,128)} %get-tuple-element.4), kind=kLoop, calls=%fused_computation | loop fusion | flops 65536 | bytes 393216 | tf_op jit(solution)/shard_map/broadcast_in_dim | solution.py:528

commit v3 on v2

--- a/solution.py
+++ b/solution.py
@@ -19,6 +19,20 @@
 def dot(a, b, dims=((1,), (0,)), precision=None):
     return lax.dot_general(
         a, b, (dims, ((), ())), precision=precision, preferred_element_type=F32
+    )
+
+
+def split(v):
+    high = v.astype(BF16)
+    return high, (v - high.astype(F32)).astype(BF16)
+
+
+def dot3(a, b, dims=((1,), (0,))):
+    (ah, al), (bh, bl) = split(a), split(b)
+    return dot(
+        jnp.concatenate([ah, ah, al], axis=dims[0][0]),
+        jnp.concatenate([bh, bl, bh], axis=dims[1][0]),
+        dims,
     )
 
 
@@ -92,7 +106,7 @@
     x, y = q // Y, lax.rem(q, Y)
     up, down = lax.rem(z + 1, Z) * 2 + c, lax.rem(z + Z - 1, Z) * 2 + c
     mate = z * 2 + 1 - c
-    peers = [(dx, dy) for dx in range(X) for dy in range(Y) if dx or dy]
+    peers = [(dx, 0) for dx in range(1, X)] + [(0, dy) for dy in range(1, Y)]
 
     def peer(dx, dy):
         return lax.rem(x + dx, X), lax.rem(y + dy, Y)
@@ -253,7 +267,7 @@
             keep = jnp.logical_and(row_lane < a_rank[0, k], col_lane < b_rank[k, j])
             core = jnp.where(keep, CO[k, g, :, at_j], 0.0)
             CO[k, g, :, at_j] = core
-            small = dot(core, PB[k, g, :, at_j], ((1,), (1,)), HIGH)
+            small = dot3(core, PB[k, g, :, at_j], ((1,), (1,)))
             SM[at, j * PW : (j + 1) * PW] = small.astype(BF16)
         return carry
 
@@ -321,6 +335,17 @@
             SF[1, j, px] = rows[halfpart:, j * PW : (j + 1) * PW]
 
     spread(0, sketch_rows, SF, SG)
+
+    for t, h in chunks:
+        for d in range(2):
+            for s in range(steps[t][d]):
+                ring_copy(t, h, d, s, z).wait_send()
+
+        def sent(o, carry):
+            mate_copy(t, h, o, c).wait_send()
+            return carry
+
+        lax.fori_loop(0, Z, sent, 0)
 
     def turn_cores(k, carry):
         for j in range(COLS):
@@ -407,7 +432,7 @@
         inverse_copy(dy, lax.rem(y + Y - dy, Y), y).wait_recv()
 
     def orthonormal(rows, j):
-        turned = dot(rows, NI[j], ((1,), (1,)), HIGH)
+        turned = dot3(rows, NI[j], ((1,), (1,)))
         lane = lax.broadcasted_iota(jnp.int32, turned.shape, 1)
         return jnp.where(lane < c_rank[0, j], turned, 0.0)
 
@@ -418,7 +443,7 @@
     def lift(k, carry):
         at = pl.ds(pl.multiple_of(k * R, R), R)
         for j in range(COLS):
-            lifted = dot(CT[k, j], PJ[at, j * PW : (j + 1) * PW], precision=HIGH)
+            lifted = dot3(CT[k, j], PJ[at, j * PW : (j + 1) * PW])
             LT[at, j * PW : (j + 1) * PW] = lifted.astype(BF16)
         return carry
 
@@ -436,6 +461,23 @@
                 CF[1, h, px, :, at_j] = rows[h * small_part + cut : (h + 1) * small_part, :]
 
     spread(1, coeff_rows, CF, CG)
+
+    def exchange_sent(i, F, G, T, U):
+        for p in range(2):
+            for d in range(1, size[p]):
+                first_copy(i, F, G, p, d).wait_send()
+            for d in range(1, size[1 - p]):
+                second_copy(i, T, U, p, d).wait_send()
+
+    exchange_sent(0, SF, SG, ST, SU)
+    for p in range(2):
+        for step in range(2):
+            for d in range(1, size[p if step == 0 else 1 - p]):
+                share_copy(step, p, d, x, y).wait_send()
+    for dx in range(1, X):
+        gram_copy(dx).wait_send()
+    for dy in range(1, Y):
+        inverse_copy(dy, y, y).wait_send()
     for j in range(COLS):
         at_q = pl.ds(pl.multiple_of(lax.rem(y, Y // 2) * small_part, small_part), small_part)
         own = orthonormal(QB[j, x, y // (Y // 2), at_q, :].astype(F32), j)
@@ -445,29 +487,7 @@
         cut = small_part // 2
         w_out[p * cut : (p + 1) * cut, :] = final(1, CT2, CU, p)
 
-    for t, h in chunks:
-        for d in range(2):
-            for s in range(steps[t][d]):
-                ring_copy(t, h, d, s, z).wait_send()
-
-        def sent(o, carry):
-            mate_copy(t, h, o, c).wait_send()
-            return carry
-
-        lax.fori_loop(0, Z, sent, 0)
-    for p in range(2):
-        for i, (F, G, T, U) in enumerate(((SF, SG, ST, SU), (CF, CG, CT2, CU))):
-            for d in range(1, size[p]):
-                first_copy(i, F, G, p, d).wait_send()
-            for d in range(1, size[1 - p]):
-                second_copy(i, T, U, p, d).wait_send()
-        for step in range(2):
-            for d in range(1, size[p if step == 0 else 1 - p]):
-                share_copy(step, p, d, x, y).wait_send()
-    for dx in range(1, X):
-        gram_copy(dx).wait_send()
-    for dy in range(1, Y):
-        inverse_copy(dy, y, y).wait_send()
+    exchange_sent(1, CF, CG, CT2, CU)
 
 
 def per_device(Z, X, Y, a_left, a_right, a_rank, b_left, b_right, b_rank, c_rank, probes):

time: 116 us -> 112 us (0.966)
  Pallas kernels: 114 us -> 109 us
    pallas_call x1, Pallas kernels: 114 us -> 109 us  [per_device(): pl.pallas_call(functools.partial(kernel, Z, X, Y), out_shape=(out, out),...]
where the time goes in v3:
time: 112 us; the launch traced here: 111 us
  Pallas kernels  109 us (97%)
  other arithmetic  1.63 us (1%)
    pallas_call x1, Pallas kernels, per_device(): pl.pallas_call(functools.partial(kernel, Z, X, Y), out_shape=(out, out),...  109 us

profile of v3, /device:TPU:2, one launch (start us, length us, event | category | flops | bytes accessed | tf_op | source)
XLA Modules:
  0.0 111.4 jit_solution(7483642213186376078)
XLA Ops:
  0.6 109.2 %shard_map.95 = (f32[64,512]{1,0:T(8,128)}, f32[64,512]{1,0:T(8,128)}) custom-call(s32[1,4]{1,0:T(1,128)} %a_rank.1, s32[4,4]{1,0:T(4,128)} %b_rank.1, s32[1,4]{1,0:T(1,128)} %c_rank.1, bf16[1,4,1024,128]{3,2,1,0:T(8,128)(2,1)} %al_hbm.1, bf16[1,4,1024,128]{3,2,1,0:T(8,128)(2,1)} %ar_hbm.1, bf16[4,4,32,128]{3,2,1,0:T(8,128)(2,1)} %bl_hbm.1, ...), custom_call_target="tpu_custom_call" | custom-call | tf_op jit(solution)/shard_map/pallas_call | solution.py:506
  109.8 1.6 %convert_bitcast_fusion = (bf16[1,64,512]{2,1,0:T(8,128)(2,1)}, bf16[1,64,512]{2,1,0:T(8,128)(2,1)}) fusion(f32[64,512]{1,0:T(8,128)} %get-tuple-element.5, f32[64,512]{1,0:T(8,128)} %get-tuple-element.4), kind=kLoop, calls=%fused_computation | loop fusion | flops 65536 | bytes 393216 | tf_op jit(solution)/shard_map/broadcast_in_dim | solution.py:548
